TPU v7x, 32 devices: a whole 2x2x4 slice. The times are simulated.
32 devices in a mesh: group: 4 (over y, core), member: 8 (over z, x).
Axes of the slice: x: 2, y: 2, z: 4, core: 2. Of those that a mesh axis runs over, the one named last changes fastest.
Arguments:
- features: bfloat16 [16384, 128], P(('group', 'member')), may hold values from -6 to 6
- edge_tiles: bfloat16 [8192, 128, 128], P(('group', 'member')), may hold values from -0.09375 to 0.09375
- tile_slot: int32 [32, 256], P(('group', 'member')), may hold values from 0 to 7
- tile_column: int32 [32, 256], P(('group', 'member')), may hold values from 0 to 31
- mirror_count: int32 [32, 4], P(('group', 'member')), may hold values from 0 to 2, as said below
- mirror_block: int32 [32, 4, 2], P(('group', 'member')), may hold values from 0 to 3, as said below
- weight_first: bfloat16 [128, 256], replicated, may hold values from -0.5 to 0.5
- bias_first: float32 [256], replicated, may hold values from -3 to 3
- weight_second: bfloat16 [256, 256], replicated, may hold values from -0.375 to 0.375
- bias_second: float32 [256], replicated, may hold values from -3 to 3
Outputs:
- layer_out: bfloat16 [16384, 256], P(('group', 'member'))
Inputs may be any that keep to these rules, and one draw needn't show every extreme that they name: `mirror_count`: at most 2 live mirror slots of one device for one destination group. `mirror_block`: the 2 entries of one device and destination group are distinct.
All inputs are finite; a program needn't handle non-finite values.
Results may differ from a plain program's by a relative error of at most 0.01.
Values may be sent and summed in bfloat16 or wider, within the bound.
A program may use at most 64 MiB of HBM per device.

v0:
```python
import math
import jax
import jax.numpy as jnp
from jax import lax
from jax.sharding import PartitionSpec as P


def expand(owners, block_count):
    return (owners[..., None] == jnp.arange(block_count)[None, None, :]).astype(jnp.bfloat16)


def fold_tiles(sources, edge_tiles, slot_ids, column_ids, alive_mask, slot_total):
    tile_total = edge_tiles.shape[0]
    tile_size = edge_tiles.shape[1]
    channels = sources.shape[2]
    block_tiles = math.gcd(tile_total, 32)
    rounds = tile_total // block_tiles
    tile_sets = edge_tiles.reshape(rounds, block_tiles, tile_size, tile_size)
    slot_sets = slot_ids.reshape(rounds, block_tiles)
    column_sets = column_ids.reshape(rounds, block_tiles)
    alive_sets = alive_mask.astype(jnp.float32).reshape(rounds, block_tiles)

    def advance(totals, pieces):
        tile_set, column_set, slot_set, alive_set = pieces
        source = jnp.take(sources, column_set, axis=0)
        products = jnp.einsum("tij,tjf->tif", tile_set, source, preferred_element_type=jnp.float32)
        return (totals.at[slot_set].add(products * alive_set[:, None, None]), None)

    start = jnp.zeros((slot_total, tile_size, channels), jnp.float32)
    totals, _ = lax.scan(advance, start, (tile_sets, column_sets, slot_sets, alive_sets))
    return totals.astype(jnp.bfloat16)


def body(
    features,
    edge_tiles,
    tile_slot,
    tile_column,
    mirror_count,
    mirror_block,
    weight_first,
    bias_first,
    weight_second,
    bias_second,
):
    group_count = lax.axis_size("group")
    slot_room = mirror_block.shape[2]
    tile_size = edge_tiles.shape[1]
    block_count = features.shape[0] // tile_size
    slot_ids = tile_slot[0]
    column_ids = tile_column[0]
    counts = mirror_count[0]
    targets = mirror_block[0]
    dest_group = slot_ids // slot_room
    within = slot_ids % slot_room
    count_of = jnp.sum(
        jnp.where(dest_group[:, None] == jnp.arange(group_count)[None, :], counts[None, :], 0),
        axis=1,
    )
    alive_mask = within < count_of
    spread = expand(targets, block_count)
    slot_total = group_count * slot_room

    def reduce_rows(partials):
        channels = partials.shape[2]
        spread_sums = jnp.einsum(
            "gcb,gcif->gbif",
            spread,
            partials.reshape(group_count, slot_room, tile_size, channels),
            preferred_element_type=jnp.float32,
        )
        return lax.psum_scatter(
            spread_sums.reshape(group_count * block_count, tile_size, channels).astype(
                jnp.bfloat16
            ),
            "group",
            scatter_dimension=0,
            tiled=True,
        ).astype(jnp.float32)

    local_rows = features.reshape(block_count, tile_size, features.shape[1])
    gathered = lax.all_gather(local_rows, "member", axis=0, tiled=True)
    first_sum = reduce_rows(
        fold_tiles(gathered, edge_tiles, slot_ids, column_ids, alive_mask, slot_total)
    ).astype(jnp.bfloat16)
    flat = first_sum.reshape(-1, first_sum.shape[2])
    result = jnp.maximum(
        jnp.dot(flat, weight_first, preferred_element_type=jnp.float32) + bias_first, 0.0
    )
    hidden = result.astype(jnp.bfloat16).reshape(first_sum.shape[0], tile_size, -1)
    sources = lax.all_gather(hidden, "member", axis=0, tiled=True)
    second = reduce_rows(
        fold_tiles(sources, edge_tiles, slot_ids, column_ids, alive_mask, slot_total)
    ).astype(jnp.bfloat16)
    flat_second = second.reshape(block_count * tile_size, -1)
    return (
        jnp.dot(flat_second, weight_second, preferred_element_type=jnp.float32) + bias_second
    ).astype(jnp.bfloat16)


def solution(mesh):
    placed = (
        P(("group", "member"), None),
        P(("group", "member"), None, None),
        P(("group", "member"), None),
        P(("group", "member"), None),
        P(("group", "member"), None),
        P(("group", "member"), None, None),
        P(),
        P(),
        P(),
        P(),
    )
    return jax.shard_map(
        body, mesh=mesh, in_specs=placed, out_specs=P(("group", "member"), None), check_vma=False
    )
```

profile of v0, /device:TPU:0, one launch (start us, length us, event | category | flops | bytes accessed | tf_op | source)
XLA Modules:
  0.0 324.9 jit_solution(12725843926485415464)
XLA Ops:
  13.1 39.3 %all-gather.3.cloned.1.call-done = bf16[32,128,128]{2,1,0:T(8,128)(2,1)} async-done(((bf16[4,128,128]{2,1,0:T(8,128)(2,1)}), bf16[32,128,128]{2,1,0:T(8,128)(2,1)}) %all-gather.3.cloned.1.call-update) | async-done | bytes 1048592 | tf_op jit(solution)/shard_map/all_gather | solution.py:82
  52.4 62.0 %while.20 = (s32[]{:T(128)}, f32[8,128,128]{2,1,0:T(8,128)S(1)}, s32[8,32]{1,0:T(8,128)S(1)}, bf16[8,32,128,128]{3,2,1,0:T(8,128)(2,1)}, s32[8,32]{1,0:T(8,128)S...) while((s32[]{:T(128)}, f32[8,128,128]{2,1,0:T(8,128)S(1)}, s32[8,32]{1,0:T(8,128)S(1)}, ...), condition=%wide.region_3.4_spmd, body=%wide.region_1.3_spmd.sunk | while | flops 135792000 | bytes 12589089 | solution.py:30
  52.5 2.9 gather_fusion
  60.2 2.9 gather_fusion
  67.9 2.9 gather_fusion
  75.7 2.9 gather_fusion
  83.4 2.9 gather_fusion
  88.5 2.7 scatter_fusion
  91.2 2.9 gather_fusion
  98.9 2.9 gather_fusion
  104.0 2.7 scatter_fusion
  106.7 2.9 gather_fusion
  116.0 20.5 %reduce-scatter.3.cloned.1.call-done = bf16[4,128,128]{2,1,0:T(8,128)(2,1)} async-done(((bf16[16,128,128]{2,1,0:T(8,128)(2,1)}), bf16[4,128,128]{2,1,0:T(8,128)(2,1)}) %reduce-scatter.3.cloned.1.call-update) | async-done | bytes 131088 | tf_op jit(solution)/shard_map/reduce_scatter | solution.py:72
  138.4 49.8 %all-gather.5.cloned.1.call-done = bf16[32,128,256]{2,1,0:T(8,128)(2,1)} async-done(((bf16[4,128,256]{2,1,0:T(8,128)(2,1)}), bf16[32,128,256]{2,1,0:T(8,128)(2,1)}) %all-gather.5.cloned.1.call-update) | async-done | bytes 2097168 | tf_op jit(solution)/shard_map/all_gather | solution.py:91
  188.3 102.1 %while.21 = (s32[]{:T(128)}, f32[8,128,256]{2,1,0:T(8,128)S(1)}, s32[8,32]{1,0:T(8,128)S(1)}, bf16[8,32,128,128]{3,2,1,0:T(8,128)(2,1)}, s32[8,32]{1,0:T(8,128)S...) while((s32[]{:T(128)}, f32[8,128,256]{2,1,0:T(8,128)S(1)}, s32[8,32]{1,0:T(8,128)S(1)}, ...), condition=%wide.region_7.8_spmd, body=%wide.region_5.7_spmd.sunk | while | flops 271582592 | bytes 24123424 | solution.py:30
  190.7 3.9 %convolution_multiply_fusion.5 = f32[32,128,256]{2,1,0:T(8,128)} fusion(f32[32]{0:T(128)S(1)} %fusion.53, bf16[32,128,256]{2,1,0:T(8,128)(2,1)S(1)} %gather_fusion.1, pred[32]{0:T(512)(128)(4,1)S(1)} %compare_and_fusion.5, bf16[8,32,128,128]{3,2,1,0:T(8,128)(2,1)} %get-tuple-element.250, s32[]{:T(128)} %get-tuple-element.239), kind=kOutput, calls=%fused_computation.24.clone.1 | convolution fusion | flops 270532608 | bytes 7340704 | tf_op jit(solution)/shard_map/while/body/eval_jaxpr/tij,tjf->tif/dot_general | solution.py:26
  194.6 6.4 %scatter_fusion.1 = f32[8,128,256]{2,1,0:T(8,128)S(1)} fusion(f32[8,128,256]{2,1,0:T(8,128)S(1)} %get-tuple-element.240, s32[32]{0:T(128)S(1)} %get-tuple-element.205, f32[32,128,256]{2,1,0:T(8,128)} %convolution_multiply_fusion.5), kind=kCustom, calls=%fused_computation.3.clone.1 | custom fusion | flops 1048576 | bytes 12583040 | tf_op jit(solution)/shard_map/while/body/eval_jaxpr/scatter-add | solution.py:27
  203.4 3.9 %convolution_multiply_fusion.5 = f32[32,128,256]{2,1,0:T(8,128)} fusion(f32[32]{0:T(128)S(1)} %fusion.53, bf16[32,128,256]{2,1,0:T(8,128)(2,1)S(1)} %gather_fusion.1, pred[32]{0:T(512)(128)(4,1)S(1)} %compare_and_fusion.5, bf16[8,32,128,128]{3,2,1,0:T(8,128)(2,1)} %get-tuple-element.250, s32[]{:T(128)} %get-tuple-element.239), kind=kOutput, calls=%fused_computation.24.clone.1 | convolution fusion | flops 270532608 | bytes 7340704 | tf_op jit(solution)/shard_map/while/body/eval_jaxpr/tij,tjf->tif/dot_general | solution.py:26
  207.3 6.4 %scatter_fusion.1 = f32[8,128,256]{2,1,0:T(8,128)S(1)} fusion(f32[8,128,256]{2,1,0:T(8,128)S(1)} %get-tuple-element.240, s32[32]{0:T(128)S(1)} %get-tuple-element.205, f32[32,128,256]{2,1,0:T(8,128)} %convolution_multiply_fusion.5), kind=kCustom, calls=%fused_computation.3.clone.1 | custom fusion | flops 1048576 | bytes 12583040 | tf_op jit(solution)/shard_map/while/body/eval_jaxpr/scatter-add | solution.py:27
  216.2 3.9 %convolution_multiply_fusion.5 = f32[32,128,256]{2,1,0:T(8,128)} fusion(f32[32]{0:T(128)S(1)} %fusion.53, bf16[32,128,256]{2,1,0:T(8,128)(2,1)S(1)} %gather_fusion.1, pred[32]{0:T(512)(128)(4,1)S(1)} %compare_and_fusion.5, bf16[8,32,128,128]{3,2,1,0:T(8,128)(2,1)} %get-tuple-element.250, s32[]{:T(128)} %get-tuple-element.239), kind=kOutput, calls=%fused_computation.24.clone.1 | convolution fusion | flops 270532608 | bytes 7340704 | tf_op jit(solution)/shard_map/while/body/eval_jaxpr/tij,tjf->tif/dot_general | solution.py:26
  220.1 6.5 %scatter_fusion.1 = f32[8,128,256]{2,1,0:T(8,128)S(1)} fusion(f32[8,128,256]{2,1,0:T(8,128)S(1)} %get-tuple-element.240, s32[32]{0:T(128)S(1)} %get-tuple-element.205, f32[32,128,256]{2,1,0:T(8,128)} %convolution_multiply_fusion.5), kind=kCustom, calls=%fused_computation.3.clone.1 | custom fusion | flops 1048576 | bytes 12583040 | tf_op jit(solution)/shard_map/while/body/eval_jaxpr/scatter-add | solution.py:27
  228.9 3.9 %convolution_multiply_fusion.5 = f32[32,128,256]{2,1,0:T(8,128)} fusion(f32[32]{0:T(128)S(1)} %fusion.53, bf16[32,128,256]{2,1,0:T(8,128)(2,1)S(1)} %gather_fusion.1, pred[32]{0:T(512)(128)(4,1)S(1)} %compare_and_fusion.5, bf16[8,32,128,128]{3,2,1,0:T(8,128)(2,1)} %get-tuple-element.250, s32[]{:T(128)} %get-tuple-element.239), kind=kOutput, calls=%fused_computation.24.clone.1 | convolution fusion | flops 270532608 | bytes 7340704 | tf_op jit(solution)/shard_map/while/body/eval_jaxpr/tij,tjf->tif/dot_general | solution.py:26
  232.9 6.5 %scatter_fusion.1 = f32[8,128,256]{2,1,0:T(8,128)S(1)} fusion(f32[8,128,256]{2,1,0:T(8,128)S(1)} %get-tuple-element.240, s32[32]{0:T(128)S(1)} %get-tuple-element.205, f32[32,128,256]{2,1,0:T(8,128)} %convolution_multiply_fusion.5), kind=kCustom, calls=%fused_computation.3.clone.1 | custom fusion | flops 1048576 | bytes 12583040 | tf_op jit(solution)/shard_map/while/body/eval_jaxpr/scatter-add | solution.py:27
  241.7 3.9 %convolution_multiply_fusion.5 = f32[32,128,256]{2,1,0:T(8,128)} fusion(f32[32]{0:T(128)S(1)} %fusion.53, bf16[32,128,256]{2,1,0:T(8,128)(2,1)S(1)} %gather_fusion.1, pred[32]{0:T(512)(128)(4,1)S(1)} %compare_and_fusion.5, bf16[8,32,128,128]{3,2,1,0:T(8,128)(2,1)} %get-tuple-element.250, s32[]{:T(128)} %get-tuple-element.239), kind=kOutput, calls=%fused_computation.24.clone.1 | convolution fusion | flops 270532608 | bytes 7340704 | tf_op jit(solution)/shard_map/while/body/eval_jaxpr/tij,tjf->tif/dot_general | solution.py:26
  245.6 6.4 %scatter_fusion.1 = f32[8,128,256]{2,1,0:T(8,128)S(1)} fusion(f32[8,128,256]{2,1,0:T(8,128)S(1)} %get-tuple-element.240, s32[32]{0:T(128)S(1)} %get-tuple-element.205, f32[32,128,256]{2,1,0:T(8,128)} %convolution_multiply_fusion.5), kind=kCustom, calls=%fused_computation.3.clone.1 | custom fusion | flops 1048576 | bytes 12583040 | tf_op jit(solution)/shard_map/while/body/eval_jaxpr/scatter-add | solution.py:27
  254.4 3.9 %convolution_multiply_fusion.5 = f32[32,128,256]{2,1,0:T(8,128)} fusion(f32[32]{0:T(128)S(1)} %fusion.53, bf16[32,128,256]{2,1,0:T(8,128)(2,1)S(1)} %gather_fusion.1, pred[32]{0:T(512)(128)(4,1)S(1)} %compare_and_fusion.5, bf16[8,32,128,128]{3,2,1,0:T(8,128)(2,1)} %get-tuple-element.250, s32[]{:T(128)} %get-tuple-element.239), kind=kOutput, calls=%fused_computation.24.clone.1 | convolution fusion | flops 270532608 | bytes 7340704 | tf_op jit(solution)/shard_map/while/body/eval_jaxpr/tij,tjf->tif/dot_general | solution.py:26
  258.4 6.4 %scatter_fusion.1 = f32[8,128,256]{2,1,0:T(8,128)S(1)} fusion(f32[8,128,256]{2,1,0:T(8,128)S(1)} %get-tuple-element.240, s32[32]{0:T(128)S(1)} %get-tuple-element.205, f32[32,128,256]{2,1,0:T(8,128)} %convolution_multiply_fusion.5), kind=kCustom, calls=%fused_computation.3.clone.1 | custom fusion | flops 1048576 | bytes 12583040 | tf_op jit(solution)/shard_map/while/body/eval_jaxpr/scatter-add | solution.py:27
  267.2 3.9 %convolution_multiply_fusion.5 = f32[32,128,256]{2,1,0:T(8,128)} fusion(f32[32]{0:T(128)S(1)} %fusion.53, bf16[32,128,256]{2,1,0:T(8,128)(2,1)S(1)} %gather_fusion.1, pred[32]{0:T(512)(128)(4,1)S(1)} %compare_and_fusion.5, bf16[8,32,128,128]{3,2,1,0:T(8,128)(2,1)} %get-tuple-element.250, s32[]{:T(128)} %get-tuple-element.239), kind=kOutput, calls=%fused_computation.24.clone.1 | convolution fusion | flops 270532608 | bytes 7340704 | tf_op jit(solution)/shard_map/while/body/eval_jaxpr/tij,tjf->tif/dot_general | solution.py:26
  271.1 6.5 %scatter_fusion.1 = f32[8,128,256]{2,1,0:T(8,128)S(1)} fusion(f32[8,128,256]{2,1,0:T(8,128)S(1)} %get-tuple-element.240, s32[32]{0:T(128)S(1)} %get-tuple-element.205, f32[32,128,256]{2,1,0:T(8,128)} %convolution_multiply_fusion.5), kind=kCustom, calls=%fused_computation.3.clone.1 | custom fusion | flops 1048576 | bytes 12583040 | tf_op jit(solution)/shard_map/while/body/eval_jaxpr/scatter-add | solution.py:27
  279.9 3.9 %convolution_multiply_fusion.5 = f32[32,128,256]{2,1,0:T(8,128)} fusion(f32[32]{0:T(128)S(1)} %fusion.53, bf16[32,128,256]{2,1,0:T(8,128)(2,1)S(1)} %gather_fusion.1, pred[32]{0:T(512)(128)(4,1)S(1)} %compare_and_fusion.5, bf16[8,32,128,128]{3,2,1,0:T(8,128)(2,1)} %get-tuple-element.250, s32[]{:T(128)} %get-tuple-element.239), kind=kOutput, calls=%fused_computation.24.clone.1 | convolution fusion | flops 270532608 | bytes 7340704 | tf_op jit(solution)/shard_map/while/body/eval_jaxpr/tij,tjf->tif/dot_general | solution.py:26
  283.9 6.5 %scatter_fusion.1 = f32[8,128,256]{2,1,0:T(8,128)S(1)} fusion(f32[8,128,256]{2,1,0:T(8,128)S(1)} %get-tuple-element.240, s32[32]{0:T(128)S(1)} %get-tuple-element.205, f32[32,128,256]{2,1,0:T(8,128)} %convolution_multiply_fusion.5), kind=kCustom, calls=%fused_computation.3.clone.1 | custom fusion | flops 1048576 | bytes 12583040 | tf_op jit(solution)/shard_map/while/body/eval_jaxpr/scatter-add | solution.py:27
  292.9 23.6 %reduce-scatter.5.cloned.1.call-done = bf16[4,128,256]{2,1,0:T(8,128)(2,1)} async-done(((bf16[16,128,256]{2,1,0:T(8,128)(2,1)}), bf16[4,128,256]{2,1,0:T(8,128)(2,1)}) %reduce-scatter.5.cloned.1.call-update) | async-done | bytes 262160 | tf_op jit(solution)/shard_map/reduce_scatter | solution.py:72
  (122 shorter events, 65.7 us)
Async XLA Ops:
  6.5 309.9 %copy-start = (bf16[256,256]{1,0:T(8,128)(2,1)S(1)}, bf16[256,256]{1,0:T(8,128)(2,1)}, u32[]{:S(2)}) copy-start(bf16[256,256]{1,0:T(8,128)(2,1)} %param.22) | copy-start | bytes 393220
  6.5 45.8 %all-gather.3.cloned.1.call-start = ((), (), s32[]{:S(2)}) async-start(), calls=%async_computation.2 | async-start | bytes 1179648 | tf_op jit(solution)/shard_map/all_gather | solution.py:82
  7.3 129.3 %reduce-scatter.3.cloned.1.call-start = ((), (), s32[]{:S(2)}) async-start(), calls=%async_computation.3 | async-start | bytes 655360 | tf_op jit(solution)/shard_map/reduce_scatter | solution.py:72
  114.4 22.2 %copy-start.1 = (bf16[128,256]{1,0:T(8,128)(2,1)S(1)}, bf16[128,256]{1,0:T(8,128)(2,1)}, u32[]{:S(2)}) copy-start(bf16[128,256]{1,0:T(8,128)(2,1)} %param.20) | copy-start | bytes 196612
  114.4 22.1 %copy-start.2 = (f32[256]{0:T(256)S(1)}, f32[256]{0:T(256)}, u32[]{:S(2)}) copy-start(f32[256]{0:T(256)} %param.21) | copy-start | bytes 3076
  116.0 72.2 %all-gather.5.cloned.1.call-start = ((), (), s32[]{:S(2)}) async-start(), calls=%async_computation.4 | async-start | bytes 2359296 | tf_op jit(solution)/shard_map/all_gather | solution.py:91
  138.4 178.1 %reduce-scatter.5.cloned.1.call-start = ((), (), s32[]{:S(2)}) async-start(), calls=%async_computation.5 | async-start | bytes 1310720 | tf_op jit(solution)/shard_map/reduce_scatter | solution.py:72
  291.7 24.8 %copy-start.3 = (f32[256]{0:T(256)S(1)}, f32[256]{0:T(256)}, u32[]{:S(2)}) copy-start(f32[256]{0:T(256)} %param.23) | copy-start | bytes 3076
Sparse Core Ops, SparseCore 0:
  9.5 42.8 all-gather.2
  116.1 20.4 reduce-scatter.2
  138.9 49.2 all-gather.4
  293.0 23.4 reduce-scatter.4
where the time goes:
time: 327 us; the launch traced here: 325 us
  waiting for transfers between devices  134 us (41%)
  other arithmetic  77.7 us (24%)
  matrix products  53.4 us (16%)
  local copies, waits for them, and re-layouts  45.6 us (14%)
  between operations  13.2 us (4%)
    scatter-add x16, other arithmetic, advance(): return (totals.at[slot_set].add(products * alive_set[:, None, None]), None)  72.9 us
    all_gather x1, waiting for transfers between devices, body(): sources = lax.all_gather(hidden, 'member', axis=0, tiled=True)  49.8 us
    dot_general x16, matrix products, advance(): jnp.einsum('tij,tjf->tif', tile_set, source, preferred_element_type=jnp.f...  47.9 us
    reduce_scatter x2, waiting for transfers between devices, reduce_rows(): lax.psum_scatter(spread_sums.reshape(group_count * block_count, tile_size...  44.1 us
    gather x16, local copies, waits for them, and re-layouts, advance(): source = jnp.take(sources, column_set, axis=0)  41.7 us
    all_gather x1, waiting for transfers between devices, body(): gathered = lax.all_gather(local_rows, 'member', axis=0, tiled=True)  39.3 us
  transfers between devices with their start and end apart: 4, of which 4 were waited for; matrix products, arithmetic and copies ran while one was open for 2% of the time, Pallas kernels for 0%

commit v1 on v0

--- a/solution.py
+++ b/solution.py
@@ -3,6 +3,27 @@
 import jax.numpy as jnp
 from jax import lax
 from jax.sharding import PartitionSpec as P
+
+
+def step_on_loads_on_mesh(chunk, dim_at):
+    chunk = jnp.moveaxis(chunk, 0, dim_at)
+    y2 = chunk.shape
+    r1 = chunk.reshape(*y2[:dim_at], y2[dim_at] * y2[dim_at + 1], *y2[dim_at + 2 :])
+    return r1
+
+
+def _carry_zone(u_in, axis_name):
+    u1, frame_out = (lax.axis_size(axis_name), lax.axis_index(axis_name))
+    long_array, reached = (u_in[None], 1)
+    while reached < u1:
+        y_new = lax.ppermute(
+            long_array, axis_name, [(dev_i, dev_i ^ reached) for dev_i in range(u1)]
+        )
+        v_next = frame_out & reached == 0
+        found_now = jnp.where(v_next, long_array, y_new)
+        long_array = jnp.concatenate([found_now, jnp.where(v_next, y_new, long_array)])
+        reached *= 2
+    return long_array
 
 
 def expand(owners, block_count):
@@ -88,7 +109,8 @@
         jnp.dot(flat, weight_first, preferred_element_type=jnp.float32) + bias_first, 0.0
     )
     hidden = result.astype(jnp.bfloat16).reshape(first_sum.shape[0], tile_size, -1)
-    sources = lax.all_gather(hidden, "member", axis=0, tiled=True)
+    all_rows = _carry_zone(hidden, "member")
+    sources = step_on_loads_on_mesh(all_rows, 0)
     second = reduce_rows(
         fold_tiles(sources, edge_tiles, slot_ids, column_ids, alive_mask, slot_total)
     ).astype(jnp.bfloat16)

time: 327 us -> 347 us (1.061)
  waiting for transfers between devices: 134 us -> 148 us
  starting transfers between devices: 0.12 us -> 5.62 us
    ppermute x0 -> x3, waiting for transfers between devices: none -> 62 us  [_carry_zone(): lax.ppermute(long_array, axis_name, [(dev_i, dev_i ^ reached) for dev_i i...]
    all_gather x1 -> x0, waiting for transfers between devices: 49.8 us -> none  [body(): sources = lax.all_gather(hidden, 'member', axis=0, tiled=True)]
    ppermute x0 -> x3, starting transfers between devices: none -> 5.54 us  [_carry_zone(): lax.ppermute(long_array, axis_name, [(dev_i, dev_i ^ reached) for dev_i i...]
  transfers between devices with their start and end apart: 4 -> 6, of which waited for: 4 -> 6; matrix products, arithmetic and copies ran while one was open for 2% -> 2% of each run, Pallas kernels for 0% -> 0%
where the time goes in v1:
time: 347 us; the launch traced here: 345 us
  waiting for transfers between devices  148 us (43%)
  other arithmetic  79.4 us (23%)
  matrix products  52.8 us (15%)
  local copies, waits for them, and re-layouts  45.5 us (13%)
  between operations  13.2 us (4%)
  starting transfers between devices  5.62 us (2%)
    scatter-add x16, other arithmetic, advance(): return (totals.at[slot_set].add(products * alive_set[:, None, None]), None)  72.9 us
    ppermute x3, waiting for transfers between devices, _carry_zone(): lax.ppermute(long_array, axis_name, [(dev_i, dev_i ^ reached) for dev_i i...  62 us
    dot_general x16, matrix products, advance(): jnp.einsum('tij,tjf->tif', tile_set, source, preferred_element_type=jnp.f...  48 us
    reduce_scatter x2, waiting for transfers between devices, reduce_rows(): lax.psum_scatter(spread_sums.reshape(group_count * block_count, tile_size...  45.5 us
    gather x16, local copies, waits for them, and re-layouts, advance(): source = jnp.take(sources, column_set, axis=0)  41.6 us
    all_gather x1, waiting for transfers between devices, body(): gathered = lax.all_gather(local_rows, 'member', axis=0, tiled=True)  39.4 us
  transfers between devices with their start and end apart: 6, of which 6 were waited for; matrix products, arithmetic and copies ran while one was open for 2% of the time, Pallas kernels for 0%

profile of v1, /device:TPU:0, one launch (start us, length us, event | category | flops | bytes accessed | tf_op | source)
XLA Modules:
  0.0 345.1 jit_solution(8583607423105681311)
XLA Ops:
  13.0 39.4 %all-gather.2.cloned.1.call-done = bf16[32,128,128]{2,1,0:T(8,128)(2,1)} async-done(((bf16[4,128,128]{2,1,0:T(8,128)(2,1)}), bf16[32,128,128]{2,1,0:T(8,128)(2,1)}) %all-gather.2.cloned.1.call-update) | async-done | bytes 1048592 | tf_op jit(solution)/shard_map/all_gather | solution.py:103
  52.4 61.8 %while.20 = (s32[]{:T(128)}, f32[8,128,128]{2,1,0:T(8,128)S(1)}, s32[8,32]{1,0:T(8,128)S(1)}, bf16[8,32,128,128]{3,2,1,0:T(8,128)(2,1)}, s32[8,32]{1,0:T(8,128)S...) while((s32[]{:T(128)}, f32[8,128,128]{2,1,0:T(8,128)S(1)}, s32[8,32]{1,0:T(8,128)S(1)}, ...), condition=%wide.region_3.4_spmd, body=%wide.region_1.3_spmd.sunk | while | flops 135792000 | bytes 12589089 | solution.py:51
  52.4 2.9 gather_fusion
  60.2 2.9 gather_fusion
  67.9 2.9 gather_fusion
  75.6 2.9 gather_fusion
  83.4 2.9 gather_fusion
  91.1 2.9 gather_fusion
  98.8 2.9 gather_fusion
  106.6 2.9 gather_fusion
  115.9 20.5 %reduce-scatter.3.cloned.1.call-done = bf16[4,128,128]{2,1,0:T(8,128)(2,1)} async-done(((bf16[16,128,128]{2,1,0:T(8,128)(2,1)}), bf16[4,128,128]{2,1,0:T(8,128)(2,1)}) %reduce-scatter.3.cloned.1.call-update) | async-done | bytes 131088 | tf_op jit(solution)/shard_map/reduce_scatter | solution.py:93
  139.1 6.6 %collective-permute-done = bf16[1,4,128,256]{3,2,1,0:T(8,128)(2,1)S(1)} collective-permute-done((bf16[1,4,128,256]{3,2,1,0:T(8,128)(2,1)S(1)}, bf16[1,4,128,256]{3,2,1,0:T(8,128)(2,1)S(1)}, u32[]{:S(2)}, u32[]{:S(2)}) %collective-permute-start) | collective-permute-done | bytes 262176 | tf_op jit(solution)/shard_map/ppermute | solution.py:19
  147.3 11.3 %collective-permute-done.1 = bf16[2,4,128,256]{3,2,1,0:T(8,128)(2,1)S(1)} collective-permute-done((bf16[2,4,128,256]{3,2,1,0:T(8,128)(2,1)S(1)}, bf16[2,4,128,256]{3,2,1,0:T(8,128)(2,1)S(1)}, u32[]{:S(2)}, u32[]{:S(2)}) %collective-permute-start.1) | collective-permute-done | bytes 524320 | tf_op jit(solution)/shard_map/ppermute | solution.py:19
  161.3 44.1 %collective-permute-done.2 = bf16[4,4,128,256]{3,2,1,0:T(8,128)(2,1)S(1)} collective-permute-done((bf16[4,4,128,256]{3,2,1,0:T(8,128)(2,1)S(1)}, bf16[4,4,128,256]{3,2,1,0:T(8,128)(2,1)S(1)}, u32[]{:S(2)}, u32[]{:S(2)}) %collective-permute-start.2) | collective-permute-done | bytes 1048608 | tf_op jit(solution)/shard_map/ppermute | solution.py:19
  207.1 102.1 %while.21 = (s32[]{:T(128)}, f32[8,128,256]{2,1,0:T(8,128)S(1)}, s32[8,32]{1,0:T(8,128)S(1)}, bf16[8,32,128,128]{3,2,1,0:T(8,128)(2,1)}, s32[8,32]{1,0:T(8,128)S...) while((s32[]{:T(128)}, f32[8,128,256]{2,1,0:T(8,128)S(1)}, s32[8,32]{1,0:T(8,128)S(1)}, ...), condition=%wide.region_7.8_spmd, body=%wide.region_5.7_spmd.sunk | while | flops 271582592 | bytes 24123424 | solution.py:51
  209.5 3.9 %convolution_multiply_fusion.5 = f32[32,128,256]{2,1,0:T(8,128)} fusion(f32[32]{0:T(128)S(1)} %fusion.53, bf16[32,128,256]{2,1,0:T(8,128)(2,1)S(1)} %gather_fusion.1, pred[32]{0:T(512)(128)(4,1)S(1)} %compare_and_fusion.5, bf16[8,32,128,128]{3,2,1,0:T(8,128)(2,1)} %get-tuple-element.256, s32[]{:T(128)} %get-tuple-element.245), kind=kOutput, calls=%fused_computation.24.clone.1 | convolution fusion | flops 270532608 | bytes 7340704 | tf_op jit(solution)/shard_map/while/body/eval_jaxpr/tij,tjf->tif/dot_general | solution.py:47
  213.4 6.4 %scatter_fusion.1 = f32[8,128,256]{2,1,0:T(8,128)S(1)} fusion(f32[8,128,256]{2,1,0:T(8,128)S(1)} %get-tuple-element.246, s32[32]{0:T(128)S(1)} %get-tuple-element.211, f32[32,128,256]{2,1,0:T(8,128)} %convolution_multiply_fusion.5), kind=kCustom, calls=%fused_computation.3.clone.1 | custom fusion | flops 1048576 | bytes 12583040 | tf_op jit(solution)/shard_map/while/body/eval_jaxpr/scatter-add | solution.py:48
  222.2 3.9 %convolution_multiply_fusion.5 = f32[32,128,256]{2,1,0:T(8,128)} fusion(f32[32]{0:T(128)S(1)} %fusion.53, bf16[32,128,256]{2,1,0:T(8,128)(2,1)S(1)} %gather_fusion.1, pred[32]{0:T(512)(128)(4,1)S(1)} %compare_and_fusion.5, bf16[8,32,128,128]{3,2,1,0:T(8,128)(2,1)} %get-tuple-element.256, s32[]{:T(128)} %get-tuple-element.245), kind=kOutput, calls=%fused_computation.24.clone.1 | convolution fusion | flops 270532608 | bytes 7340704 | tf_op jit(solution)/shard_map/while/body/eval_jaxpr/tij,tjf->tif/dot_general | solution.py:47
  226.2 6.4 %scatter_fusion.1 = f32[8,128,256]{2,1,0:T(8,128)S(1)} fusion(f32[8,128,256]{2,1,0:T(8,128)S(1)} %get-tuple-element.246, s32[32]{0:T(128)S(1)} %get-tuple-element.211, f32[32,128,256]{2,1,0:T(8,128)} %convolution_multiply_fusion.5), kind=kCustom, calls=%fused_computation.3.clone.1 | custom fusion | flops 1048576 | bytes 12583040 | tf_op jit(solution)/shard_map/while/body/eval_jaxpr/scatter-add | solution.py:48
  235.0 3.9 %convolution_multiply_fusion.5 = f32[32,128,256]{2,1,0:T(8,128)} fusion(f32[32]{0:T(128)S(1)} %fusion.53, bf16[32,128,256]{2,1,0:T(8,128)(2,1)S(1)} %gather_fusion.1, pred[32]{0:T(512)(128)(4,1)S(1)} %compare_and_fusion.5, bf16[8,32,128,128]{3,2,1,0:T(8,128)(2,1)} %get-tuple-element.256, s32[]{:T(128)} %get-tuple-element.245), kind=kOutput, calls=%fused_computation.24.clone.1 | convolution fusion | flops 270532608 | bytes 7340704 | tf_op jit(solution)/shard_map/while/body/eval_jaxpr/tij,tjf->tif/dot_general | solution.py:47
  238.9 6.5 %scatter_fusion.1 = f32[8,128,256]{2,1,0:T(8,128)S(1)} fusion(f32[8,128,256]{2,1,0:T(8,128)S(1)} %get-tuple-element.246, s32[32]{0:T(128)S(1)} %get-tuple-element.211, f32[32,128,256]{2,1,0:T(8,128)} %convolution_multiply_fusion.5), kind=kCustom, calls=%fused_computation.3.clone.1 | custom fusion | flops 1048576 | bytes 12583040 | tf_op jit(solution)/shard_map/while/body/eval_jaxpr/scatter-add | solution.py:48
  247.7 3.9 %convolution_multiply_fusion.5 = f32[32,128,256]{2,1,0:T(8,128)} fusion(f32[32]{0:T(128)S(1)} %fusion.53, bf16[32,128,256]{2,1,0:T(8,128)(2,1)S(1)} %gather_fusion.1, pred[32]{0:T(512)(128)(4,1)S(1)} %compare_and_fusion.5, bf16[8,32,128,128]{3,2,1,0:T(8,128)(2,1)} %get-tuple-element.256, s32[]{:T(128)} %get-tuple-element.245), kind=kOutput, calls=%fused_computation.24.clone.1 | convolution fusion | flops 270532608 | bytes 7340704 | tf_op jit(solution)/shard_map/while/body/eval_jaxpr/tij,tjf->tif/dot_general | solution.py:47
  251.7 6.5 %scatter_fusion.1 = f32[8,128,256]{2,1,0:T(8,128)S(1)} fusion(f32[8,128,256]{2,1,0:T(8,128)S(1)} %get-tuple-element.246, s32[32]{0:T(128)S(1)} %get-tuple-element.211, f32[32,128,256]{2,1,0:T(8,128)} %convolution_multiply_fusion.5), kind=kCustom, calls=%fused_computation.3.clone.1 | custom fusion | flops 1048576 | bytes 12583040 | tf_op jit(solution)/shard_map/while/body/eval_jaxpr/scatter-add | solution.py:48
  260.5 3.9 %convolution_multiply_fusion.5 = f32[32,128,256]{2,1,0:T(8,128)} fusion(f32[32]{0:T(128)S(1)} %fusion.53, bf16[32,128,256]{2,1,0:T(8,128)(2,1)S(1)} %gather_fusion.1, pred[32]{0:T(512)(128)(4,1)S(1)} %compare_and_fusion.5, bf16[8,32,128,128]{3,2,1,0:T(8,128)(2,1)} %get-tuple-element.256, s32[]{:T(128)} %get-tuple-element.245), kind=kOutput, calls=%fused_computation.24.clone.1 | convolution fusion | flops 270532608 | bytes 7340704 | tf_op jit(solution)/shard_map/while/body/eval_jaxpr/tij,tjf->tif/dot_general | solution.py:47
  264.5 6.4 %scatter_fusion.1 = f32[8,128,256]{2,1,0:T(8,128)S(1)} fusion(f32[8,128,256]{2,1,0:T(8,128)S(1)} %get-tuple-element.246, s32[32]{0:T(128)S(1)} %get-tuple-element.211, f32[32,128,256]{2,1,0:T(8,128)} %convolution_multiply_fusion.5), kind=kCustom, calls=%fused_computation.3.clone.1 | custom fusion | flops 1048576 | bytes 12583040 | tf_op jit(solution)/shard_map/while/body/eval_jaxpr/scatter-add | solution.py:48
  273.3 3.9 %convolution_multiply_fusion.5 = f32[32,128,256]{2,1,0:T(8,128)} fusion(f32[32]{0:T(128)S(1)} %fusion.53, bf16[32,128,256]{2,1,0:T(8,128)(2,1)S(1)} %gather_fusion.1, pred[32]{0:T(512)(128)(4,1)S(1)} %compare_and_fusion.5, bf16[8,32,128,128]{3,2,1,0:T(8,128)(2,1)} %get-tuple-element.256, s32[]{:T(128)} %get-tuple-element.245), kind=kOutput, calls=%fused_computation.24.clone.1 | convolution fusion | flops 270532608 | bytes 7340704 | tf_op jit(solution)/shard_map/while/body/eval_jaxpr/tij,tjf->tif/dot_general | solution.py:47
  277.2 6.4 %scatter_fusion.1 = f32[8,128,256]{2,1,0:T(8,128)S(1)} fusion(f32[8,128,256]{2,1,0:T(8,128)S(1)} %get-tuple-element.246, s32[32]{0:T(128)S(1)} %get-tuple-element.211, f32[32,128,256]{2,1,0:T(8,128)} %convolution_multiply_fusion.5), kind=kCustom, calls=%fused_computation.3.clone.1 | custom fusion | flops 1048576 | bytes 12583040 | tf_op jit(solution)/shard_map/while/body/eval_jaxpr/scatter-add | solution.py:48
  286.0 3.9 %convolution_multiply_fusion.5 = f32[32,128,256]{2,1,0:T(8,128)} fusion(f32[32]{0:T(128)S(1)} %fusion.53, bf16[32,128,256]{2,1,0:T(8,128)(2,1)S(1)} %gather_fusion.1, pred[32]{0:T(512)(128)(4,1)S(1)} %compare_and_fusion.5, bf16[8,32,128,128]{3,2,1,0:T(8,128)(2,1)} %get-tuple-element.256, s32[]{:T(128)} %get-tuple-element.245), kind=kOutput, calls=%fused_computation.24.clone.1 | convolution fusion | flops 270532608 | bytes 7340704 | tf_op jit(solution)/shard_map/while/body/eval_jaxpr/tij,tjf->tif/dot_general | solution.py:47
  290.0 6.5 %scatter_fusion.1 = f32[8,128,256]{2,1,0:T(8,128)S(1)} fusion(f32[8,128,256]{2,1,0:T(8,128)S(1)} %get-tuple-element.246, s32[32]{0:T(128)S(1)} %get-tuple-element.211, f32[32,128,256]{2,1,0:T(8,128)} %convolution_multiply_fusion.5), kind=kCustom, calls=%fused_computation.3.clone.1 | custom fusion | flops 1048576 | bytes 12583040 | tf_op jit(solution)/shard_map/while/body/eval_jaxpr/scatter-add | solution.py:48
  298.8 3.9 %convolution_multiply_fusion.5 = f32[32,128,256]{2,1,0:T(8,128)} fusion(f32[32]{0:T(128)S(1)} %fusion.53, bf16[32,128,256]{2,1,0:T(8,128)(2,1)S(1)} %gather_fusion.1, pred[32]{0:T(512)(128)(4,1)S(1)} %compare_and_fusion.5, bf16[8,32,128,128]{3,2,1,0:T(8,128)(2,1)} %get-tuple-element.256, s32[]{:T(128)} %get-tuple-element.245), kind=kOutput, calls=%fused_computation.24.clone.1 | convolution fusion | flops 270532608 | bytes 7340704 | tf_op jit(solution)/shard_map/while/body/eval_jaxpr/tij,tjf->tif/dot_general | solution.py:47
  302.7 6.5 %scatter_fusion.1 = f32[8,128,256]{2,1,0:T(8,128)S(1)} fusion(f32[8,128,256]{2,1,0:T(8,128)S(1)} %get-tuple-element.246, s32[32]{0:T(128)S(1)} %get-tuple-element.211, f32[32,128,256]{2,1,0:T(8,128)} %convolution_multiply_fusion.5), kind=kCustom, calls=%fused_computation.3.clone.1 | custom fusion | flops 1048576 | bytes 12583040 | tf_op jit(solution)/shard_map/while/body/eval_jaxpr/scatter-add | solution.py:48
  311.7 25.0 %reduce-scatter.5.cloned.1.call-done = bf16[4,128,256]{2,1,0:T(8,128)(2,1)} async-done(((bf16[16,128,256]{2,1,0:T(8,128)(2,1)}), bf16[4,128,256]{2,1,0:T(8,128)(2,1)}) %reduce-scatter.5.cloned.1.call-update) | async-done | bytes 262160 | tf_op jit(solution)/shard_map/reduce_scatter | solution.py:93
  (131 shorter events, 77.5 us)
Async XLA Ops:
  6.5 330.2 %copy-start = (bf16[256,256]{1,0:T(8,128)(2,1)S(1)}, bf16[256,256]{1,0:T(8,128)(2,1)}, u32[]{:S(2)}) copy-start(bf16[256,256]{1,0:T(8,128)(2,1)} %param.22) | copy-start | bytes 393220
  6.5 45.8 %all-gather.2.cloned.1.call-start = ((), (), s32[]{:S(2)}) async-start(), calls=%async_computation.2 | async-start | bytes 1179648 | tf_op jit(solution)/shard_map/all_gather | solution.py:103
  7.3 129.2 %reduce-scatter.3.cloned.1.call-start = ((), (), s32[]{:S(2)}) async-start(), calls=%async_computation.3 | async-start | bytes 655360 | tf_op jit(solution)/shard_map/reduce_scatter | solution.py:93
  114.3 22.2 %copy-start.1 = (bf16[128,256]{1,0:T(8,128)(2,1)S(1)}, bf16[128,256]{1,0:T(8,128)(2,1)}, u32[]{:S(2)}) copy-start(bf16[128,256]{1,0:T(8,128)(2,1)} %param.20) | copy-start | bytes 196612
  114.3 22.1 %copy-start.2 = (f32[256]{0:T(256)S(1)}, f32[256]{0:T(256)}, u32[]{:S(2)}) copy-start(f32[256]{0:T(256)} %param.21) | copy-start | bytes 3076
  115.8 220.9 %reduce-scatter.5.cloned.1.call-start = ((), (), s32[]{:S(2)}) async-start(), calls=%async_computation.4 | async-start | bytes 1310720 | tf_op jit(solution)/shard_map/reduce_scatter | solution.py:93
  137.5 8.1 %collective-permute-start = (bf16[1,4,128,256]{3,2,1,0:T(8,128)(2,1)S(1)}, bf16[1,4,128,256]{3,2,1,0:T(8,128)(2,1)S(1)}, u32[]{:S(2)}, u32[]{:S(2)}) collective-permute-start(bf16[1,4,128,256]{3,2,1,0:T(8,128)(2,1)S(1)} %bitcast.86), channel_id=1, source_target_pairs={{0,1},{1,0},{2,3},{3,2},{4,5},{5,4},{6,7},{7,6},{8,9},{9,8},{10,11... | collective-permute-start | bytes 786440 | tf_op jit(solution)/shard_map/ppermute | solution.py:19
  145.8 12.9 %collective-permute-start.1 = (bf16[2,4,128,256]{3,2,1,0:T(8,128)(2,1)S(1)}, bf16[2,4,128,256]{3,2,1,0:T(8,128)(2,1)S(1)}, u32[]{:S(2)}, u32[]{:S(2)}) collective-permute-start(bf16[2,4,128,256]{3,2,1,0:T(8,128)(2,1)S(1)} %pad_maximum_fusion.2), channel_id=1, source_target_pairs={{0,2},{1,3},{2,0},{3,1},{4,6},{5,7},{6,4},{7,5},{8,10},{9,11},{10,... | collective-permute-start | bytes 1572872 | tf_op jit(solution)/shard_map/ppermute | solution.py:19
  158.8 46.6 %collective-permute-start.2 = (bf16[4,4,128,256]{3,2,1,0:T(8,128)(2,1)S(1)}, bf16[4,4,128,256]{3,2,1,0:T(8,128)(2,1)S(1)}, u32[]{:S(2)}, u32[]{:S(2)}) collective-permute-start(bf16[4,4,128,256]{3,2,1,0:T(8,128)(2,1)S(1)} %pad_maximum_fusion.1), channel_id=1, source_target_pairs={{0,4},{1,5},{2,6},{3,7},{4,0},{5,1},{6,2},{7,3},{8,12},{9,13},{10,... | collective-permute-start | bytes 3145736 | tf_op jit(solution)/shard_map/ppermute | solution.py:19
  310.5 26.2 %copy-start.3 = (f32[256]{0:T(256)S(1)}, f32[256]{0:T(256)}, u32[]{:S(2)}) copy-start(f32[256]{0:T(256)} %param.23) | copy-start | bytes 3076
Sparse Core Ops, SparseCore 0:
  9.5 42.8 all-gather.1
  116.0 20.4 reduce-scatter.2
  311.8 24.8 reduce-scatter.4
